TPU v7x, 256 devices: a whole 4x4x8 slice. The times are simulated.
256 devices in a mesh: mic: 4 (over y), seq: 64 (over z, x, core).
Axes of the slice: x: 4, y: 4, z: 8, core: 2. Of those that a mesh axis runs over, the one named last changes fastest.
Arguments:
- frames_in: bfloat16 [8, 32768, 512], P('mic', 'seq'), may hold values from -16 to 16
- w_qkv: bfloat16 [8, 512, 1536], P('mic'), may hold values from -0.25 to 0.25
- w_join: bfloat16 [4096, 1024], P(('mic', 'seq')), may hold values from -0.09375 to 0.09375
- norm_gain: float32 [1024], replicated, may hold values from 0.5 to 2
- w_router: bfloat16 [1024, 64], replicated, may hold values from -0.1875 to 0.1875
- w_gate: bfloat16 [64, 1024, 4096], P('seq', None, 'mic'), may hold values from -0.1875 to 0.1875
- w_up: bfloat16 [64, 1024, 4096], P('seq', None, 'mic'), may hold values from -0.1875 to 0.1875
- w_down: bfloat16 [64, 4096, 1024], P('seq', 'mic'), may hold values from -0.09375 to 0.09375
- expert_ids: int32 [64, 4, 128, 2], P('seq', 'mic'), may hold values from 0 to 63, all different within a row; in each aligned block of 128 rows (0 to 127, 128 to 255, ..., all dimensions but the last counted through in order) at most 6 rows name the same one
Outputs:
- layer_out: bfloat16 [64, 4, 128, 1024], P('seq', 'mic')
Inputs may be any that keep to these rules, and one draw needn't show every extreme that they name: `expert_ids`: in the rows of one block (128 frames) no expert is named more than 6 times, a bound that some block reaches; the two ids of a frame differ.
All inputs are finite; a program needn't handle non-finite values.
Results may differ from a plain program's by a relative error of at most 0.017.
Values may be sent and summed in bfloat16 or wider, within the bound.
A program may use at most 128 MiB of HBM per device.

v0:
```python
import jax
import jax.numpy as jnp
from jax import lax
from jax.sharding import PartitionSpec as P

MICS = 8
HEADS = 8
TOP = 2


def body(frames_in, w_qkv, w_join, norm_gain, w_router, w_gate, w_up, w_down, expert_ids):
    mic_count = lax.axis_size("mic")
    seq_count = lax.axis_size("seq")
    mic_local, span, chan_width = frames_in.shape
    frame_rows = span // mic_count
    head_dim = chan_width // HEADS
    model_width = w_join.shape[1]
    expert_count = w_router.shape[1]
    exp_local = w_gate.shape[0]
    capacity = max(2, 3 * TOP * frame_rows // (2 * expert_count))
    projected = jnp.einsum(
        "mfc,mce->mfe", frames_in, w_qkv, preferred_element_type=jnp.float32
    ).astype(jnp.bfloat16)
    projected = projected.reshape(mic_local, mic_count, frame_rows, 3 * chan_width)
    arrived_block = lax.all_to_all(projected, "mic", split_axis=1, concat_axis=0, tiled=True)
    arrived_block = arrived_block[:, 0]
    frame_count = arrived_block.shape[1]
    queries = arrived_block[..., :chan_width].reshape(MICS, frame_count, HEADS, head_dim)
    keys_all = arrived_block[..., chan_width : 2 * chan_width].reshape(
        MICS, frame_count, HEADS, head_dim
    )
    values_all = arrived_block[..., 2 * chan_width :].reshape(MICS, frame_count, HEADS, head_dim)
    scores = jnp.einsum(
        "ifhd,jfhd->fhij", queries, keys_all, preferred_element_type=jnp.float32
    ) * head_dim ** (-0.5)
    row_max = jnp.max(scores, axis=-1, keepdims=True)
    weights = jnp.exp(scores - row_max)
    probs = (weights / jnp.sum(weights, axis=-1, keepdims=True)).astype(jnp.bfloat16)
    mixed_heads = jnp.einsum(
        "fhij,jfhd->fihd", probs, values_all, preferred_element_type=jnp.float32
    )
    attended = mixed_heads.astype(jnp.bfloat16).reshape(frame_count, MICS * chan_width)
    joined = jnp.dot(
        attended,
        lax.all_gather(w_join, ("mic", "seq"), axis=0, tiled=True),
        preferred_element_type=jnp.float32,
    )
    scale_row = lax.rsqrt(jnp.mean(joined * joined, axis=-1, keepdims=True) + 1e-06)
    normed = (joined * scale_row * norm_gain).astype(jnp.bfloat16)
    logits = jnp.dot(normed, w_router, preferred_element_type=jnp.float32)
    expert_rows = expert_ids.reshape(frame_rows, TOP)
    chosen = (expert_rows[..., None] == jnp.arange(expert_count, dtype=jnp.int32)).astype(jnp.int32)
    picked = jnp.sum(logits[:, None, :] * chosen.astype(jnp.float32), axis=-1)
    first_gate = 1.0 / (1.0 + jnp.exp(picked[:, 1] - picked[:, 0]))
    gates = jnp.stack([first_gate, 1.0 - first_gate], axis=-1)
    counts = jnp.sum(chosen, axis=1)
    before = jnp.cumsum(counts, axis=0) - counts
    slot_index = jnp.sum(before[:, None, :] * chosen, axis=-1)
    in_slot = slot_index[..., None] == jnp.arange(capacity, dtype=jnp.int32)
    mapped = (
        ((chosen[..., :, None] == 1) & in_slot[..., None, :])
        .reshape(frame_rows, TOP, expert_count * capacity)
        .astype(jnp.bfloat16)
    )
    merged_map = jnp.sum(mapped, axis=1)
    buffers = jnp.einsum(
        "rs,rd->sd", merged_map, normed, preferred_element_type=jnp.float32
    ).astype(jnp.bfloat16)
    buffers = buffers.reshape(seq_count, exp_local * capacity, model_width)
    landed = lax.all_to_all(buffers, "seq", split_axis=0, concat_axis=0, tiled=True)
    arrived = lax.all_gather(landed[None], "mic", axis=0, tiled=True)
    flat = arrived.reshape(mic_count * seq_count * exp_local * capacity, model_width)
    piece_rows = flat.reshape(-1, exp_local, capacity, model_width)
    first_proj = jnp.einsum(
        "nejd,edf->nejf", piece_rows, w_gate, preferred_element_type=jnp.float32
    )
    second_proj = jnp.einsum("nejd,edf->nejf", piece_rows, w_up, preferred_element_type=jnp.float32)
    inner = (jax.nn.silu(first_proj) * second_proj).astype(jnp.bfloat16)
    result = jnp.einsum("nejf,efd->nejd", inner, w_down, preferred_element_type=jnp.float32)
    summed = lax.psum_scatter(
        result.reshape(
            lax.axis_size("mic") * (seq_count * exp_local * capacity), model_width
        ).astype(jnp.bfloat16),
        "mic",
        scatter_dimension=0,
        tiled=True,
    ).astype(jnp.float32)
    summed = summed.astype(jnp.bfloat16).reshape(seq_count, exp_local * capacity, model_width)
    returned = lax.all_to_all(summed, "seq", split_axis=0, concat_axis=0, tiled=True)
    returned = returned.reshape(expert_count * capacity, model_width)
    picked_out = jnp.einsum("rks,sd->rkd", mapped, returned, preferred_element_type=jnp.float32)
    total = joined + jnp.sum(gates[..., None] * picked_out, axis=1)
    return total.astype(jnp.bfloat16).reshape(1, 1, frame_rows, model_width)


def solution(mesh):
    return jax.shard_map(
        body,
        mesh=mesh,
        in_specs=(
            P("mic", "seq", None),
            P("mic", None, None),
            P(("mic", "seq"), None),
            P(),
            P(),
            P("seq", None, "mic"),
            P("seq", None, "mic"),
            P("seq", "mic", None),
            P("seq", "mic", None, None),
        ),
        out_specs=P("seq", "mic", None, None),
        check_vma=False,
    )
```

profile of v0, /device:TPU:1, one launch (start us, length us, event | category | flops | bytes accessed | tf_op | source)
XLA Modules:
  0.0 346.4 jit_solution(7928431488291336185)
XLA Ops:
  8.4 3.0 convolution_convert_fusion
  11.5 2.0 copy.26
  13.4 5.1 %all-to-all-start = ((bf16[2,4,128,1536]{3,2,0,1:T(8,128)(2,1)}), bf16[2,4,128,1536]{3,2,0,1:T(8,128)(2,1)S(1)}, u32[]{:S(2)}, u32[]{:S(2)}) async-start(bf16[2,4,128,1536]{3,2,0,1:T(8,128)(2,1)} %copy.26), calls=%async_computation | async-start | bytes 6291456 | tf_op jit(solution)/shard_map/all_to_all | solution.py:25
  19.2 35.4 %all-to-all-done = bf16[2,4,128,1536]{3,2,0,1:T(8,128)(2,1)S(1)} async-done(((bf16[2,4,128,1536]{3,2,0,1:T(8,128)(2,1)}), bf16[2,4,128,1536]{3,2,0,1:T(8,128)(2,1)S(1)}, u32[]{:S(2)}, u32[]{:S(2)}) %all-to-all-start) | async-done | bytes 3145760 | tf_op jit(solution)/shard_map/all_to_all | solution.py:25
  58.1 3.8 %copy.30 = bf16[8,128,8,64]{3,0,2,1:T(8,128)(2,1)} copy(bf16[8,128,8,64]{1,3,2,0:T(8,128)(2,1)S(1)} %bitcast.103) | data formatting | bytes 2097152 | tf_op jit(solution)/shard_map/reshape | solution.py:28
  62.5 3.7 %copy.31 = bf16[8,128,8,64]{3,0,2,1:T(8,128)(2,1)} copy(bf16[8,128,8,64]{1,3,2,0:T(8,128)(2,1)S(1)} %bitcast.104) | data formatting | bytes 2097152 | tf_op jit(solution)/shard_map/reshape | solution.py:29
  66.9 3.7 %copy.32 = bf16[8,128,8,64]{3,0,2,1:T(8,128)(2,1)} copy(bf16[8,128,8,64]{1,3,2,0:T(8,128)(2,1)S(1)} %bitcast.105) | data formatting | bytes 2097152 | tf_op jit(solution)/shard_map/reshape | solution.py:32
  70.6 6.6 %fusion.38 = (f32[128,8,8]{2,1,0:T(8,128)S(1)}, f32[128,8,8,8]{2,3,1,0:T(8,128)}) fusion(bf16[8,128,8,64]{3,0,2,1:T(8,128)(2,1)S(1)} %copy-done.5, bf16[8,128,8,64]{3,0,2,1:T(8,128)(2,1)} %copy.31), kind=kOutput, calls=%fused_computation.56 | convolution fusion | flops 8585223 | bytes 2392064 | tf_op jit(solution)/shard_map/sub | solution.py:37
  77.2 4.7 %convert_bitcast_fusion.1 = bf16[128,8,8,64]{3,1,2,0:T(8,128)(2,1)} fusion(bf16[8,128,8,64]{3,0,2,1:T(8,128)(2,1)} %copy.32, f32[128,8,8,8]{2,3,1,0:T(8,128)} %get-tuple-element.11, f32[128,8,8]{2,1,0:T(8,128)S(1)} %get-tuple-element.10), kind=kOutput, calls=%fused_computation.22 | convolution fusion | flops 9043968 | bytes 2392064 | tf_op jit(solution)/shard_map/fhij,jfhd->fihd/dot_general | solution.py:39
  81.9 3.2 copy.34
  85.1 59.5 %all-gather.4.cloned.1.call-done = bf16[4096,1024]{1,0:T(8,128)(2,1)} async-done(((bf16[16,1024]{1,0:T(8,128)(2,1)}), bf16[4096,1024]{1,0:T(8,128)(2,1)}) %all-gather.4.cloned.1.call-update) | async-done | bytes 8388624 | tf_op jit(solution)/shard_map/all_gather | solution.py:45
  144.6 4.7 %multiply_reduce_fusion.1 = (f32[128]{0:T(128)S(1)}, f32[128,1024]{1,0:T(8,128)S(1)}) fusion(bf16[128,4096]{0,1:T(8,128)(2,1)S(1)} %bitcast.102, bf16[4096,1024]{1,0:T(8,128)(2,1)} %all-gather.4.cloned.1.call-done), kind=kOutput, calls=%fused_computation.33 | convolution fusion | flops 1074003840 | bytes 9961984 | tf_op jit(solution)/shard_map/dot_general | solution.py:43
  150.0 35.1 %all_to_all.25 = bf16[64,6,1024]{2,1,0:T(8,128)(2,1)S(1)} all-to-all(bf16[64,6,1024]{2,1,0:T(8,128)(2,1)S(1)} %reshape.92), channel_id=1, replica_groups=mesh['mic'=4,'seq'=64] {'seq'}, dimensions={0} | all-to-all | bytes 1572864 | tf_op jit(solution)/shard_map/all_to_all | solution.py:70
  186.5 37.7 %all-gather.6.cloned.1.call-done = bf16[256,6,1024]{2,0,1:T(8,128)(2,1)} async-done(((bf16[64,6,1024]{2,0,1:T(8,128)(2,1)}), bf16[256,6,1024]{2,0,1:T(8,128)(2,1)}) %all-gather.6.cloned.1.call-update) | async-done | bytes 3145744 | tf_op jit(solution)/shard_map/all_gather | solution.py:71
  224.2 8.6 %fusion.19 = f32[256,6,1024]{2,0,1:T(8,128)} fusion(bf16[256,6,1024]{2,0,1:T(8,128)(2,1)} %all-gather.6.cloned.1.call-done, bf16[1,1024,1024]{2,1,0:T(8,128)(2,1)} %param.14), kind=kOutput, calls=%fused_computation.20 | convolution fusion | flops 3221225472 | bytes 11534336 | tf_op jit(solution)/shard_map/nejd,edf->nejf/dot_general | solution.py:74
  232.8 10.6 %convert_bitcast_fusion = bf16[256,1,6,1024]{3,0,2,1:T(8,128)(2,1)S(1)} fusion(f32[256,6,1024]{2,0,1:T(8,128)} %fusion.19, bf16[256,6,1024]{2,0,1:T(8,128)(2,1)} %all-gather.6.cloned.1.call-done, bf16[1,1024,1024]{2,1,0:T(8,128)(2,1)} %param.16, bf16[1,1024,1024]{2,1,0:T(8,128)(2,1)} %param.15), kind=kOutput, calls=%fused_computation.15 | convolution fusion | flops 6453460992 | bytes 16777216 | tf_op jit(solution)/shard_map/nejf,efd->nejd/dot_general | solution.py:79
  243.4 3.7 %copy.40 = bf16[256,1,6,1024]{3,2,0,1:T(8,128)(2,1)} copy(bf16[256,1,6,1024]{3,0,2,1:T(8,128)(2,1)S(1)} %convert_bitcast_fusion) | data formatting | bytes 6291456 | tf_op jit(solution)/shard_map/convert_element_type | solution.py:83
  247.1 6.3 %convert_element_type.71 = bf16[1536,1024]{1,0:T(8,128)(2,1)} reshape(bf16[256,1,6,1024]{3,2,0,1:T(8,128)(2,1)} %copy.40) | data formatting | bytes 6291456 | tf_op jit(solution)/shard_map/convert_element_type | solution.py:83
  253.5 41.3 %reduce-scatter.2.cloned.1.call-done = bf16[384,1024]{1,0:T(8,128)(2,1)} async-done(((bf16[1536,1024]{1,0:T(8,128)(2,1)}), bf16[384,1024]{1,0:T(8,128)(2,1)}) %reduce-scatter.2.cloned.1.call-update) | async-done | bytes 786448 | tf_op jit(solution)/shard_map/reduce_scatter | solution.py:80
  294.7 2.3 reshape.98
  297.1 10.8 %all-to-all-start.2 = ((bf16[64,6,1024]{2,1,0:T(8,128)(2,1)}), bf16[64,6,1024]{2,1,0:T(8,128)(2,1)}, u32[]{:S(2)}, u32[]{:S(2)}) async-start(bf16[64,6,1024]{2,1,0:T(8,128)(2,1)} %reshape.98), calls=%async_computation.3 | async-start | bytes 2097152 | tf_op jit(solution)/shard_map/all_to_all | solution.py:89
  309.3 26.5 %all-to-all-done.2 = bf16[64,6,1024]{2,1,0:T(8,128)(2,1)} async-done(((bf16[64,6,1024]{2,1,0:T(8,128)(2,1)}), bf16[64,6,1024]{2,1,0:T(8,128)(2,1)}, u32[]{:S(2)}, u32[]{:S(2)}) %all-to-all-start.2) | async-done | bytes 786464 | tf_op jit(solution)/shard_map/all_to_all | solution.py:89
  335.8 2.3 fusion.24
  338.1 1.8 fusion.28
  (47 shorter events, 10.7 us)
Async XLA Ops:
  6.5 1.9 copy-start
  6.5 138.0 %all-gather.4.cloned.1.call-start = ((), (), s32[]{:S(2)}) async-start(), calls=%async_computation.4 | async-start | bytes 8421376 | tf_op jit(solution)/shard_map/all_gather | solution.py:45
  13.4 5.2 %copy-start.8 = (s32[1,1,128,2]{2,3,1,0:T(2,128)S(1)}, s32[1,1,128,2]{2,3,1,0:T(2,128)}, u32[]{:S(2)}) copy-start(s32[1,1,128,2]{2,3,1,0:T(2,128)} %param.17) | copy-start | bytes 3076
  13.4 41.2 %all-to-all-start = ((bf16[2,4,128,1536]{3,2,0,1:T(8,128)(2,1)}), bf16[2,4,128,1536]{3,2,0,1:T(8,128)(2,1)S(1)}, u32[]{:S(2)}, u32[]{:S(2)}) async-start(bf16[2,4,128,1536]{3,2,0,1:T(8,128)(2,1)} %copy.26), calls=%async_computation | async-start | bytes 6291456 | tf_op jit(solution)/shard_map/all_to_all | solution.py:25
  18.6 205.6 %all-gather.6.cloned.1.call-start = ((), (), s32[]{:S(2)}) async-start(), calls=%async_computation.6 | async-start | bytes 3932160 | tf_op jit(solution)/shard_map/all_gather | solution.py:71
  56.4 5.5 %copy-start.4 = (bf16[8,128,512]{2,1,0:T(8,128)(2,1)S(1)}, bf16[8,128,512]{2,1,0:T(8,128)(2,1)}, u32[]{:S(2)}) copy-start(bf16[8,128,512]{2,1,0:T(8,128)(2,1)} %get-tuple-element.7) | copy-start | bytes 3145732
  61.8 4.4 %copy-start.3 = (bf16[8,128,512]{2,1,0:T(8,128)(2,1)S(1)}, bf16[8,128,512]{2,1,0:T(8,128)(2,1)}, u32[]{:S(2)}) copy-start(bf16[8,128,512]{2,1,0:T(8,128)(2,1)} %get-tuple-element.9) | copy-start | bytes 3145732
  66.9 3.8 %copy-start.5 = (bf16[8,128,8,64]{3,0,2,1:T(8,128)(2,1)S(1)}, bf16[8,128,8,64]{3,0,2,1:T(8,128)(2,1)}, u32[]{:S(2)}) copy-start(bf16[8,128,8,64]{3,0,2,1:T(8,128)(2,1)} %copy.30) | copy-start | bytes 3145732
  144.6 4.8 %copy-start.7 = (f32[1024]{0:T(1024)S(1)}, f32[1024]{0:T(1024)}, u32[]{:S(2)}) copy-start(f32[1024]{0:T(1024)} %param.12) | copy-start | bytes 12292
  149.3 37.1 %copy-start.2 = (f32[128,1024]{1,0:T(8,128)}, f32[128,1024]{1,0:T(8,128)S(1)}, u32[]{:S(2)}) copy-start(f32[128,1024]{1,0:T(8,128)S(1)} %get-tuple-element.13) | copy-start | bytes 1572868
  186.5 108.3 %reduce-scatter.2.cloned.1.call-start = ((), (), s32[]{:S(2)}) async-start(), calls=%async_computation.5 | async-start | bytes 3932160 | tf_op jit(solution)/shard_map/reduce_scatter | solution.py:80
  253.4 54.4 %copy-start.6 = (bf16[1024,64]{0,1:T(8,128)(2,1)S(1)}, bf16[1024,64]{0,1:T(8,128)(2,1)}, u32[]{:S(2)}) copy-start(bf16[1024,64]{0,1:T(8,128)(2,1)} %param.13) | copy-start | bytes 393220
  294.7 45.2 %copy-start.1 = (bf16[2,512,1536]{2,1,0:T(8,128)(2,1)S(1)}, bf16[2,512,1536]{2,1,0:T(8,128)(2,1)}, u32[]{:S(2)}) copy-start(bf16[2,512,1536]{2,1,0:T(8,128)(2,1)} %param.10) | copy-start | bytes 9437188
  297.1 38.7 %all-to-all-start.2 = ((bf16[64,6,1024]{2,1,0:T(8,128)(2,1)}), bf16[64,6,1024]{2,1,0:T(8,128)(2,1)}, u32[]{:S(2)}, u32[]{:S(2)}) async-start(bf16[64,6,1024]{2,1,0:T(8,128)(2,1)} %reshape.98), calls=%async_computation.3 | async-start | bytes 2097152 | tf_op jit(solution)/shard_map/all_to_all | solution.py:89
Sparse Core Ops, SparseCore 0:
  10.9 133.5 all-gather.3
  186.6 37.5 all-gather.5
  253.6 41.0 reduce-scatter.1
where the time goes:
time: 347 us; the launch traced here: 346 us
  waiting for transfers between devices  201 us (58%)
  matrix products  42.3 us (12%)
  local copies, waits for them, and re-layouts  36.6 us (11%)
  blocking collectives  35.1 us (10%)
  starting transfers between devices  16 us (5%)
  between operations  13.3 us (4%)
    all_gather x1, waiting for transfers between devices, body(): lax.all_gather(w_join, ('mic', 'seq'), axis=0, tiled=True)  59.5 us
    reduce_scatter x1, waiting for transfers between devices, body(): lax.psum_scatter(result.reshape(lax.axis_size('mic') * (seq_count * exp_l...  41.3 us
    all_gather x1, waiting for transfers between devices, body(): arrived = lax.all_gather(landed[None], 'mic', axis=0, tiled=True)  37.7 us
    all_to_all x1, waiting for transfers between devices, body(): lax.all_to_all(projected, 'mic', split_axis=1, concat_axis=0, tiled=True)  35.4 us
    all_to_all x1, blocking collectives, body(): lax.all_to_all(buffers, 'seq', split_axis=0, concat_axis=0, tiled=True)  35.1 us
    all_to_all x1, waiting for transfers between devices, body(): lax.all_to_all(summed, 'seq', split_axis=0, concat_axis=0, tiled=True)  26.5 us
    all_to_all x1, starting transfers between devices, body(): lax.all_to_all(summed, 'seq', split_axis=0, concat_axis=0, tiled=True)  10.8 us
    dot_general x1, matrix products, body(): jnp.einsum('nejf,efd->nejd', inner, w_down, preferred_element_type=jnp.fl...  10.6 us
  transfers between devices with their start and end apart: 5, of which 5 were waited for; matrix products, arithmetic and copies ran while one was open for 11% of the time, Pallas kernels for 0%

commit v1 on v0

--- a/solution.py
+++ b/solution.py
@@ -68,7 +68,12 @@
     ).astype(jnp.bfloat16)
     buffers = buffers.reshape(seq_count, exp_local * capacity, model_width)
     landed = lax.all_to_all(buffers, "seq", split_axis=0, concat_axis=0, tiled=True)
-    arrived = lax.all_gather(landed[None], "mic", axis=0, tiled=True)
+    ring = [landed[None]]
+    for hop in range(3):
+        ring.append(lax.ppermute(ring[-1], "mic", [(dev, (dev + 1) % 4) for dev in range(4)]))
+    arrived = jnp.roll(
+        jnp.concatenate(ring[::-1], axis=0), (lax.axis_index("mic") + 1) * ring[0].shape[0], axis=0
+    )
     flat = arrived.reshape(mic_count * seq_count * exp_local * capacity, model_width)
     piece_rows = flat.reshape(-1, exp_local, capacity, model_width)
     first_proj = jnp.einsum(

time: 347 us -> 370 us (1.066)
  waiting for transfers between devices: 201 us -> 218 us
  local copies, waits for them, and re-layouts: 36.6 us -> 44.4 us
    ppermute x0 -> x3, waiting for transfers between devices: none -> 54 us  [body(): lax.ppermute(ring[-1], 'mic', [(dev, (dev + 1) % 4) for dev in range(4)])]
    all_gather x1 -> x0, waiting for transfers between devices: 37.7 us -> none  [body(): arrived = lax.all_gather(landed[None], 'mic', axis=0, tiled=True)]
    unnamed x18 -> x25, local copies, waits for them, and re-layouts: 1.2 us -> 6.54 us
  transfers between devices with their start and end apart: 5 -> 7, of which waited for: 5 -> 7; matrix products, arithmetic and copies ran while one was open for 11% -> 10% of each run, Pallas kernels for 0% -> 0%
where the time goes in v1:
time: 370 us; the launch traced here: 369 us
  waiting for transfers between devices  218 us (59%)
  local copies, waits for them, and re-layouts  44.4 us (12%)
  matrix products  39.8 us (11%)
  blocking collectives  35.1 us (9%)
  starting transfers between devices  16 us (4%)
  between operations  13.7 us (4%)
    all_gather x1, waiting for transfers between devices, body(): lax.all_gather(w_join, ('mic', 'seq'), axis=0, tiled=True)  59.9 us
    ppermute x3, waiting for transfers between devices, body(): lax.ppermute(ring[-1], 'mic', [(dev, (dev + 1) % 4) for dev in range(4)])  54 us
    reduce_scatter x1, waiting for transfers between devices, body(): lax.psum_scatter(result.reshape(lax.axis_size('mic') * (seq_count * exp_l...  41.6 us
    all_to_all x1, waiting for transfers between devices, body(): lax.all_to_all(projected, 'mic', split_axis=1, concat_axis=0, tiled=True)  35.4 us
    all_to_all x1, blocking collectives, body(): lax.all_to_all(buffers, 'seq', split_axis=0, concat_axis=0, tiled=True)  35.1 us
    all_to_all x1, waiting for transfers between devices, body(): lax.all_to_all(summed, 'seq', split_axis=0, concat_axis=0, tiled=True)  26.5 us
    convert_element_type x2, local copies, waits for them, and re-layouts, body(): summed = lax.psum_scatter(result.reshape(lax.axis_size('mic') * (seq_coun...  11.9 us
    dot_general x1, matrix products, body(): jnp.einsum('nejf,efd->nejd', inner, w_down, preferred_element_type=jnp.fl...  11.3 us
  transfers between devices with their start and end apart: 7, of which 7 were waited for; matrix products, arithmetic and copies ran while one was open for 10% of the time, Pallas kernels for 0%

profile of v1, /device:TPU:1, one launch (start us, length us, event | category | flops | bytes accessed | tf_op | source)
XLA Modules:
  0.0 369.4 jit_solution(3145688667992886278)
XLA Ops:
  8.4 3.0 convolution_convert_fusion
  13.4 5.1 %all-to-all-start = ((bf16[2,4,128,1536]{3,2,0,1:T(8,128)(2,1)}), bf16[2,4,128,1536]{3,2,0,1:T(8,128)(2,1)S(1)}, u32[]{:S(2)}, u32[]{:S(2)}) async-start(bf16[2,4,128,1536]{3,2,0,1:T(8,128)(2,1)} %copy.26), calls=%async_computation | async-start | bytes 6291456 | tf_op jit(solution)/shard_map/all_to_all | solution.py:25
  19.2 35.4 %all-to-all-done = bf16[2,4,128,1536]{3,2,0,1:T(8,128)(2,1)S(1)} async-done(((bf16[2,4,128,1536]{3,2,0,1:T(8,128)(2,1)}), bf16[2,4,128,1536]{3,2,0,1:T(8,128)(2,1)S(1)}, u32[]{:S(2)}, u32[]{:S(2)}) %all-to-all-start) | async-done | bytes 3145760 | tf_op jit(solution)/shard_map/all_to_all | solution.py:25
  58.2 3.7 %copy.30 = bf16[8,128,8,64]{3,0,2,1:T(8,128)(2,1)} copy(bf16[8,128,8,64]{1,3,2,0:T(8,128)(2,1)S(1)} %bitcast.108) | data formatting | bytes 2097152 | tf_op jit(solution)/shard_map/reshape | solution.py:28
  62.6 3.7 %copy.31 = bf16[8,128,8,64]{3,0,2,1:T(8,128)(2,1)} copy(bf16[8,128,8,64]{1,3,2,0:T(8,128)(2,1)S(1)} %bitcast.109) | data formatting | bytes 2097152 | tf_op jit(solution)/shard_map/reshape | solution.py:29
  67.0 3.0 copy.32
  70.0 7.2 %fusion.38 = (f32[128,8,8]{2,1,0:T(8,128)S(1)}, f32[128,8,8,8]{2,3,1,0:T(8,128)}) fusion(bf16[8,128,8,64]{3,0,2,1:T(8,128)(2,1)} %copy.30, bf16[8,128,8,64]{3,0,2,1:T(8,128)(2,1)} %copy.31), kind=kOutput, calls=%fused_computation.65 | convolution fusion | flops 8585223 | bytes 2392064 | tf_op jit(solution)/shard_map/sub | solution.py:37
  77.2 4.2 %convert_bitcast_fusion.1 = bf16[128,8,8,64]{3,1,2,0:T(8,128)(2,1)} fusion(bf16[8,128,8,64]{3,0,2,1:T(8,128)(2,1)S(1)} %copy.32, f32[128,8,8,8]{2,3,1,0:T(8,128)} %get-tuple-element.11, f32[128,8,8]{2,1,0:T(8,128)S(1)} %get-tuple-element.10), kind=kOutput, calls=%fused_computation.22 | convolution fusion | flops 9043968 | bytes 2392064 | tf_op jit(solution)/shard_map/fhij,jfhd->fihd/dot_general | solution.py:39
  81.4 3.2 copy.34
  84.6 59.9 %all-gather.2.cloned.1.call-done = bf16[4096,1024]{1,0:T(8,128)(2,1)} async-done(((bf16[16,1024]{1,0:T(8,128)(2,1)}), bf16[4096,1024]{1,0:T(8,128)(2,1)}) %all-gather.2.cloned.1.call-update) | async-done | bytes 8388624 | tf_op jit(solution)/shard_map/all_gather | solution.py:45
  144.5 4.7 %multiply_reduce_fusion.1 = (f32[128]{0:T(128)S(1)}, f32[128,1024]{1,0:T(8,128)S(1)}) fusion(bf16[128,4096]{0,1:T(8,128)(2,1)S(1)} %bitcast.107, bf16[4096,1024]{1,0:T(8,128)(2,1)} %all-gather.2.cloned.1.call-done), kind=kOutput, calls=%fused_computation.39 | convolution fusion | flops 1074003840 | bytes 9961984 | tf_op jit(solution)/shard_map/dot_general | solution.py:43
  150.4 35.1 %all_to_all.25 = bf16[64,6,1024]{2,1,0:T(8,128)(2,1)S(1)} all-to-all(bf16[64,6,1024]{2,1,0:T(8,128)(2,1)S(1)} %reshape.92), channel_id=1, replica_groups=mesh['mic'=4,'seq'=64] {'seq'}, dimensions={0} | all-to-all | bytes 1572864 | tf_op jit(solution)/shard_map/all_to_all | solution.py:70
  186.0 18.9 %collective-permute-done = bf16[1,64,6,1024]{3,1,2,0:T(8,128)(2,1)S(1)} collective-permute-done((bf16[1,64,6,1024]{3,1,2,0:T(8,128)(2,1)S(1)}, bf16[1,64,6,1024]{3,1,2,0:T(8,128)(2,1)S(1)}, u32[]{:S(2)}, u32[]{:S(2)}) %collective-permute-start) | collective-permute-done | bytes 786464 | tf_op jit(solution)/shard_map/ppermute | solution.py:73
  204.8 18.0 %collective-permute-done.1 = bf16[1,64,6,1024]{3,1,2,0:T(8,128)(2,1)S(1)} collective-permute-done((bf16[1,64,6,1024]{3,1,2,0:T(8,128)(2,1)S(1)}, bf16[1,64,6,1024]{3,1,2,0:T(8,128)(2,1)S(1)}, u32[]{:S(2)}, u32[]{:S(2)}) %collective-permute-start.1) | collective-permute-done | bytes 786464 | tf_op jit(solution)/shard_map/ppermute | solution.py:73
  222.8 17.1 %collective-permute-done.2 = bf16[1,64,6,1024]{3,1,2,0:T(8,128)(2,1)} collective-permute-done((bf16[1,64,6,1024]{3,1,2,0:T(8,128)(2,1)S(1)}, bf16[1,64,6,1024]{3,1,2,0:T(8,128)(2,1)}, u32[]{:S(2)}, u32[]{:S(2)}) %collective-permute-start.2) | collective-permute-done | bytes 786464 | tf_op jit(solution)/shard_map/ppermute | solution.py:73
  247.3 5.3 %fusion.19 = f32[256,6,1024]{2,0,1:T(8,128)} fusion(bf16[256,6,1024]{2,0,1:T(8,128)(2,1)S(1)} %bitcast.111, bf16[1,1024,1024]{2,1,0:T(8,128)(2,1)S(1)} %copy-done.8), kind=kOutput, calls=%fused_computation.20 | convolution fusion | flops 3221225472 | bytes 11534336 | tf_op jit(solution)/shard_map/nejd,edf->nejf/dot_general | solution.py:79
  252.6 11.3 %convert_bitcast_fusion = bf16[256,1,6,1024]{3,0,2,1:T(8,128)(2,1)} fusion(f32[256,6,1024]{2,0,1:T(8,128)} %fusion.19, bf16[256,6,1024]{2,0,1:T(8,128)(2,1)S(1)} %bitcast.112, bf16[1,1024,1024]{2,1,0:T(8,128)(2,1)} %param.16, bf16[1,1024,1024]{2,1,0:T(8,128)(2,1)} %param.15), kind=kOutput, calls=%fused_computation.15 | convolution fusion | flops 6453460992 | bytes 16777216 | tf_op jit(solution)/shard_map/nejf,efd->nejd/dot_general | solution.py:84
  263.9 5.6 %copy.47 = bf16[256,1,6,1024]{3,2,0,1:T(8,128)(2,1)} copy(bf16[256,1,6,1024]{3,0,2,1:T(8,128)(2,1)} %convert_bitcast_fusion) | data formatting | bytes 6291456 | tf_op jit(solution)/shard_map/convert_element_type | solution.py:88
  269.5 6.3 %convert_element_type.71 = bf16[1536,1024]{1,0:T(8,128)(2,1)} reshape(bf16[256,1,6,1024]{3,2,0,1:T(8,128)(2,1)} %copy.47) | data formatting | bytes 6291456 | tf_op jit(solution)/shard_map/convert_element_type | solution.py:88
  275.9 41.6 %reduce-scatter.2.cloned.1.call-done = bf16[384,1024]{1,0:T(8,128)(2,1)} async-done(((bf16[1536,1024]{1,0:T(8,128)(2,1)}), bf16[384,1024]{1,0:T(8,128)(2,1)}) %reduce-scatter.2.cloned.1.call-update) | async-done | bytes 786448 | tf_op jit(solution)/shard_map/reduce_scatter | solution.py:85
  317.5 2.2 reshape.98
  319.7 10.8 %all-to-all-start.2 = ((bf16[64,6,1024]{2,1,0:T(8,128)(2,1)}), bf16[64,6,1024]{2,1,0:T(8,128)(2,1)}, u32[]{:S(2)}, u32[]{:S(2)}) async-start(bf16[64,6,1024]{2,1,0:T(8,128)(2,1)} %reshape.98), calls=%async_computation.3 | async-start | bytes 2097152 | tf_op jit(solution)/shard_map/all_to_all | solution.py:94
  331.9 26.5 %all-to-all-done.2 = bf16[64,6,1024]{2,1,0:T(8,128)(2,1)} async-done(((bf16[64,6,1024]{2,1,0:T(8,128)(2,1)}), bf16[64,6,1024]{2,1,0:T(8,128)(2,1)}, u32[]{:S(2)}, u32[]{:S(2)}) %all-to-all-start.2) | async-done | bytes 786464 | tf_op jit(solution)/shard_map/all_to_all | solution.py:94
  358.4 2.3 fusion.24
  (60 shorter events, 21.3 us)
Async XLA Ops:
  6.5 1.9 copy-start
  6.5 138.0 %all-gather.2.cloned.1.call-start = ((), (), s32[]{:S(2)}) async-start(), calls=%async_computation.4 | async-start | bytes 8421376 | tf_op jit(solution)/shard_map/all_gather | solution.py:45
  13.4 5.2 %copy-start.7 = (s32[1,1,128,2]{2,3,1,0:T(2,128)S(1)}, s32[1,1,128,2]{2,3,1,0:T(2,128)}, u32[]{:S(2)}) copy-start(s32[1,1,128,2]{2,3,1,0:T(2,128)} %param.17) | copy-start | bytes 3076
  13.4 41.2 %all-to-all-start = ((bf16[2,4,128,1536]{3,2,0,1:T(8,128)(2,1)}), bf16[2,4,128,1536]{3,2,0,1:T(8,128)(2,1)S(1)}, u32[]{:S(2)}, u32[]{:S(2)}) async-start(bf16[2,4,128,1536]{3,2,0,1:T(8,128)(2,1)} %copy.26), calls=%async_computation | async-start | bytes 6291456 | tf_op jit(solution)/shard_map/all_to_all | solution.py:25
  18.6 298.9 %reduce-scatter.2.cloned.1.call-start = ((), (), s32[]{:S(2)}) async-start(), calls=%async_computation.5 | async-start | bytes 3932160 | tf_op jit(solution)/shard_map/reduce_scatter | solution.py:85
  56.5 5.5 %copy-start.4 = (bf16[8,128,512]{2,1,0:T(8,128)(2,1)S(1)}, bf16[8,128,512]{2,1,0:T(8,128)(2,1)}, u32[]{:S(2)}) copy-start(bf16[8,128,512]{2,1,0:T(8,128)(2,1)} %get-tuple-element.7) | copy-start | bytes 3145732
  58.2 8.1 %copy-start.3 = (bf16[8,128,512]{2,1,0:T(8,128)(2,1)S(1)}, bf16[8,128,512]{2,1,0:T(8,128)(2,1)}, u32[]{:S(2)}) copy-start(bf16[8,128,512]{2,1,0:T(8,128)(2,1)} %get-tuple-element.9) | copy-start | bytes 3145732
  144.5 4.8 %copy-start.6 = (f32[1024]{0:T(1024)S(1)}, f32[1024]{0:T(1024)}, u32[]{:S(2)}) copy-start(f32[1024]{0:T(1024)} %param.12) | copy-start | bytes 12292
  149.3 0.8 copy-start.2
  185.9 19.0 %collective-permute-start = (bf16[1,64,6,1024]{3,1,2,0:T(8,128)(2,1)S(1)}, bf16[1,64,6,1024]{3,1,2,0:T(8,128)(2,1)S(1)}, u32[]{:S(2)}, u32[]{:S(2)}) collective-permute-start(bf16[1,64,6,1024]{3,1,2,0:T(8,128)(2,1)S(1)} %copy.39), channel_id=1, source_target_pairs={{0,64},{64,128},{128,192},{192,0},{1,65},{65,129},{129,193},{193,1... | collective-permute-start | bytes 2359304 | tf_op jit(solution)/shard_map/ppermute | solution.py:73
  204.8 18.0 %collective-permute-start.1 = (bf16[1,64,6,1024]{3,1,2,0:T(8,128)(2,1)S(1)}, bf16[1,64,6,1024]{3,1,2,0:T(8,128)(2,1)S(1)}, u32[]{:S(2)}, u32[]{:S(2)}) collective-permute-start(bf16[1,64,6,1024]{3,1,2,0:T(8,128)(2,1)S(1)} %collective-permute-done), channel_id=1, source_target_pairs={{0,64},{64,128},{128,192},{192,0},{1,65},{65,129},{129,193},{193,1... | collective-permute-start | bytes 2359304 | tf_op jit(solution)/shard_map/ppermute | solution.py:73
  222.8 17.1 %collective-permute-start.2 = (bf16[1,64,6,1024]{3,1,2,0:T(8,128)(2,1)S(1)}, bf16[1,64,6,1024]{3,1,2,0:T(8,128)(2,1)}, u32[]{:S(2)}, u32[]{:S(2)}) collective-permute-start(bf16[1,64,6,1024]{3,1,2,0:T(8,128)(2,1)S(1)} %collective-permute-done.1), channel_id=1, source_target_pairs={{0,64},{64,128},{128,192},{192,0},{1,65},{65,129},{129,193},{193,1... | collective-permute-start | bytes 2359304 | tf_op jit(solution)/shard_map/ppermute | solution.py:73
  245.5 1.7 copy-start.8
  275.8 54.7 %copy-start.5 = (bf16[1024,64]{0,1:T(8,128)(2,1)S(1)}, bf16[1024,64]{0,1:T(8,128)(2,1)}, u32[]{:S(2)}) copy-start(bf16[1024,64]{0,1:T(8,128)(2,1)} %param.13) | copy-start | bytes 393220
  275.9 86.7 %copy-start.1 = (bf16[2,512,1536]{2,1,0:T(8,128)(2,1)S(1)}, bf16[2,512,1536]{2,1,0:T(8,128)(2,1)}, u32[]{:S(2)}) copy-start(bf16[2,512,1536]{2,1,0:T(8,128)(2,1)} %param.10) | copy-start | bytes 9437188
  319.7 38.7 %all-to-all-start.2 = ((bf16[64,6,1024]{2,1,0:T(8,128)(2,1)}), bf16[64,6,1024]{2,1,0:T(8,128)(2,1)}, u32[]{:S(2)}, u32[]{:S(2)}) async-start(bf16[64,6,1024]{2,1,0:T(8,128)(2,1)} %reshape.98), calls=%async_computation.3 | async-start | bytes 2097152 | tf_op jit(solution)/shard_map/all_to_all | solution.py:94
Sparse Core Ops, SparseCore 0:
  10.9 133.5 all-gather.1
  276.0 41.4 reduce-scatter.1
